TPU v7x, 32 devices: a whole 2x2x4 slice. The times are simulated.
32 devices in a mesh: pair: 16 (over z, x, core), virt: 2 (over y).
Axes of the slice: x: 2, y: 2, z: 4, core: 2. Of those that a mesh axis runs over, the one named last changes fastest.
Arguments:
- amplitudes: bfloat16 [96, 96, 128, 128], P('pair', None, 'virt'), may hold values from -6 to 6
- integrals: bfloat16 [128, 20, 128, 128], P('virt'), may hold values from -0.125 to 0.125
- cd_tiles: int32 [128, 20], P('virt'), may hold values from 0 to 127, as said below
- tile_counts: int32 [128], P('virt'), may hold values from 10 to 20, as said below
- eps_occ: float32 [96], replicated, may hold values from -2 to -0.5
- eps_virt: float32 [128], replicated, may hold values from 0.5 to 3
Outputs:
- new_amplitudes: bfloat16 [96, 96, 128, 128], P('pair', None, 'virt')
Inputs may be any that keep to these rules, and one draw needn't show every extreme that they name: `cd_tiles`: row a holds 20 different numbers from lo(a) to lo(a) + 2 * 64 - 1, where lo(a) = min(max(a - 64, 0), 0); only its first tile_counts[a] entries are live. `tile_counts`: some entry equals 20.
All inputs are finite; a program needn't handle non-finite values.
Results may differ from a plain program's by a relative error of at most 0.001.
Values may be sent and summed in bfloat16 or wider, within the bound.
A program may use at most 448 MiB of HBM per device.

v0:
```python
import jax
import jax.numpy as jnp
from jax import lax
from jax.sharding import PartitionSpec as P


def extended(cells, sides, width):
    for axis, dim in sides:
        count = lax.axis_size(axis)
        ends = count - 1
        head = lax.slice_in_dim(cells, 0, width, axis=dim)
        tail = lax.slice_in_dim(cells, cells.shape[dim] - width, cells.shape[dim], axis=dim)
        cells = jnp.concatenate(
            [
                lax.ppermute(tail, axis, [(i, (i + 1) % count) for i in range(ends)]),
                cells,
                lax.ppermute(head, axis, [((i + 1) % count, i) for i in range(ends)]),
            ],
            axis=dim,
        )
    return cells


def per_device(amplitudes, integrals, cd_tiles, tile_counts, eps_occ, eps_virt):
    own_rows = amplitudes.shape[0]
    own_tiles = amplitudes.shape[2]
    slot_count = integrals.shape[1]
    first_tile = lax.axis_index("virt") * own_tiles
    first_row = lax.axis_index("pair") * own_rows
    local_tiles = cd_tiles - first_tile + own_tiles
    slot_ids = lax.broadcasted_iota(jnp.int32, cd_tiles.shape, 1)
    kept_slots = (slot_ids < tile_counts[:, None]).astype(jnp.bfloat16)
    masked_weights = integrals * kept_slots[:, :, None, None]
    padded = extended(amplitudes, (("virt", 2),), own_tiles)
    block_width = min(4, slot_count)
    ladder = None
    for block_start in range(0, slot_count, block_width):
        block_stop = min(block_start + block_width, slot_count)
        columns = local_tiles[:, block_start:block_stop]
        picked = jnp.take(padded, columns, axis=2)
        weights = masked_weights[:, block_start:block_stop]
        term = jnp.einsum("ijasd,asdb->ijab", picked, weights, preferred_element_type=jnp.float32)
        ladder = term if ladder is None else ladder + term
    arrived_ladder = lax.all_to_all(
        lax.all_to_all(ladder, "pair", split_axis=1, concat_axis=0, tiled=True),
        "virt",
        split_axis=3,
        concat_axis=2,
        tiled=True,
    )
    partner = jnp.transpose(arrived_ladder, (1, 0, 3, 2))
    occupied_own = lax.dynamic_slice_in_dim(eps_occ, first_row, own_rows)
    virtual_own = lax.dynamic_slice_in_dim(eps_virt, first_tile, own_tiles)
    denominator = (
        occupied_own[:, None, None, None]
        + eps_occ[None, :, None, None]
        - virtual_own[None, None, :, None]
        - eps_virt[None, None, None, :]
    )
    return ((ladder + partner) / denominator).astype(jnp.bfloat16)


def solution(mesh):
    in_specs = (
        P("pair", None, "virt", None),
        P("virt", None, None, None),
        P("virt", None),
        P("virt"),
        P(),
        P(),
    )
    out_specs = P("pair", None, "virt", None)
    return jax.shard_map(
        per_device, mesh=mesh, in_specs=in_specs, out_specs=out_specs, check_vma=False
    )
```

profile of v0, /device:TPU:0, one launch (start us, length us, event | category | flops | bytes accessed | tf_op | source)
XLA Modules:
  0.0 1329.9 jit_solution(11712600738236134319)
XLA Ops:
  0.0 13.5 %copy.69 = bf16[6,96,64,128]{3,1,2,0:T(8,128)(2,1)} copy(bf16[6,96,64,128]{3,2,1,0:T(8,128)(2,1)} %param.8) | data formatting | bytes 18874368 | tf_op args[0]
  13.5 8.6 collective-permute-start
  22.0 1.5 collective-permute-start.1
  23.5 0.7 subtract_add_fusion
  24.2 0.1 copy.75
  24.3 0.1 reshape.119
  24.4 0.1 copy.78
  24.5 0.1 reshape.123
  24.7 0.1 copy.77
  24.8 0.7 copy.74
  25.5 0.1 copy.81
  25.6 0.1 reshape.127
  25.7 0.1 copy.84
  25.8 0.1 reshape.131
  25.9 0.7 copy.80
  26.6 0.1 copy.72
  26.7 0.1 reshape.115
  26.8 0.7 copy.68
  27.5 0.7 copy.83
  28.2 0.7 fusion.25
  29.0 28.2 %broadcast_multiply_fusion = bf16[64,20,128,128]{3,2,1,0:T(8,128)(2,1)} fusion(bf16[64,20,128,128]{3,2,1,0:T(8,128)(2,1)} %param.9, bf16[64,20]{1,0:T(8,128)(2,1)S(1)} %fusion.25), kind=kLoop, calls=%fused_computation.25 | loop fusion | flops 20971520 | bytes 83888640 | tf_op jit(solution)/shard_map/mul | solution.py:33
  57.2 163.7 %collective-permute-done = bf16[6,96,64,128]{3,1,2,0:T(8,128)(2,1)} collective-permute-done((bf16[6,96,64,128]{3,1,2,0:T(8,128)(2,1)}, bf16[6,96,64,128]{3,1,2,0:T(8,128)(2,1)}, u32[]{:S(2)}, u32[]{:S(2)}) %collective-permute-start) | collective-permute-done | bytes 9437216 | tf_op jit(solution)/shard_map/ppermute | solution.py:15
  220.9 9.0 constant_dynamic-update-slice_fusion.2
  229.9 13.3 %constant_dynamic-update-slice_fusion.1 = bf16[6,96,192,128]{3,1,2,0:T(8,128)(2,1)} fusion(bf16[6,96,192,128]{3,1,2,0:T(8,128)(2,1)} %constant_dynamic-update-slice_fusion.2, bf16[6,96,64,128]{3,2,1,0:T(8,128)(2,1)} %param.8), kind=kLoop, calls=%fused_computation.49 | loop fusion | bytes 18874368
  243.2 9.0 constant_dynamic-update-slice_fusion
  252.2 24.5 %gather_fusion.2 = bf16[256,6,96,128]{3,2,1,0:T(8,128)(2,1)} fusion(bf16[6,96,192,128]{3,1,2,0:T(8,128)(2,1)} %constant_dynamic-update-slice_fusion, s32[1024]{0:T(1024)S(1)} %get-tuple-element.18), kind=kCustom, calls=%fused_computation.2.clone | custom fusion | bytes 75498496 | tf_op jit(solution)/shard_map/jit(_take)/gather | solution.py:40
  276.7 24.5 %gather_fusion.1 = bf16[256,6,96,128]{3,2,1,0:T(8,128)(2,1)} fusion(bf16[6,96,192,128]{3,1,2,0:T(8,128)(2,1)} %constant_dynamic-update-slice_fusion, s32[1024]{0:T(1024)S(1)} %get-tuple-element.19), kind=kCustom, calls=%fused_computation.1.clone | custom fusion | bytes 75498496 | tf_op jit(solution)/shard_map/jit(_take)/gather | solution.py:40
  301.2 24.3 %gather_fusion.3 = bf16[256,6,96,128]{3,2,1,0:T(8,128)(2,1)} fusion(bf16[6,96,192,128]{3,1,2,0:T(8,128)(2,1)} %constant_dynamic-update-slice_fusion, s32[1024]{0:T(1024)S(1)} %get-tuple-element.17), kind=kCustom, calls=%fused_computation.3.clone | custom fusion | bytes 75498496 | tf_op jit(solution)/shard_map/jit(_take)/gather | solution.py:40
  325.5 24.3 %gather_fusion = bf16[256,6,96,128]{3,2,1,0:T(8,128)(2,1)} fusion(bf16[6,96,192,128]{3,1,2,0:T(8,128)(2,1)} %constant_dynamic-update-slice_fusion, s32[1024]{0:T(1024)S(1)} %pad_clamp_fusion.4), kind=kCustom, calls=%fused_computation.clone | custom fusion | bytes 75498496 | tf_op jit(solution)/shard_map/jit(_take)/gather | solution.py:40
  349.8 24.4 %gather_fusion.4 = bf16[256,6,96,128]{3,2,1,0:T(8,128)(2,1)} fusion(bf16[6,96,192,128]{3,1,2,0:T(8,128)(2,1)} %constant_dynamic-update-slice_fusion, s32[1024]{0:T(1024)S(1)} %get-tuple-element.16), kind=kCustom, calls=%fused_computation.4.clone | custom fusion | bytes 75498496 | tf_op jit(solution)/shard_map/jit(_take)/gather | solution.py:40
  374.2 22.9 %fusion.4 = f32[64,128,6,96,1]{1,3,4,2,0:T(8,128)} fusion(bf16[64,4,6,96,128]{4,3,2,1,0:T(8,128)(2,1)} %bitcast.110, pred[64,4]{1,0:T(8,128)(4,1)S(1)} %copy.77, bf16[64,20,128,128]{3,2,1,0:T(8,128)(2,1)} %broadcast_multiply_fusion), kind=kOutput, calls=%fused_computation.9 | convolution fusion | flops 4850712576 | bytes 65011968 | tf_op jit(solution)/shard_map/ijasd,asdb->ijab/dot_general | solution.py:42
  397.1 22.8 %fusion.6 = f32[64,128,6,96,1]{1,3,4,2,0:T(8,128)} fusion(bf16[64,4,6,96,128]{4,3,2,1,0:T(8,128)(2,1)} %bitcast.111, pred[64,4]{1,0:T(8,128)(4,1)S(1)} %copy-done.1, bf16[64,20,128,128]{3,2,1,0:T(8,128)(2,1)} %broadcast_multiply_fusion), kind=kOutput, calls=%fused_computation.11 | convolution fusion | flops 4850712576 | bytes 65011968 | tf_op jit(solution)/shard_map/ijasd,asdb->ijab/dot_general | solution.py:42
  419.9 23.2 %fusion.2 = f32[64,128,6,96,1]{1,3,4,2,0:T(8,128)} fusion(bf16[64,4,6,96,128]{4,3,2,1,0:T(8,128)(2,1)} %bitcast.109, pred[64,4]{1,0:T(8,128)(4,1)S(1)} %copy-done.2, bf16[64,20,128,128]{3,2,1,0:T(8,128)(2,1)} %broadcast_multiply_fusion), kind=kOutput, calls=%fused_computation.7 | convolution fusion | flops 4850712576 | bytes 65011968 | tf_op jit(solution)/shard_map/ijasd,asdb->ijab/dot_general | solution.py:42
  443.0 22.8 %fusion.8 = f32[64,128,6,96,1]{1,3,4,2,0:T(8,128)} fusion(bf16[64,4,6,96,128]{4,3,2,1,0:T(8,128)(2,1)} %bitcast.108, pred[64,4]{1,0:T(8,128)(4,1)S(1)} %copy-done.3, bf16[64,20,128,128]{3,2,1,0:T(8,128)(2,1)} %broadcast_multiply_fusion), kind=kOutput, calls=%fused_computation.13 | convolution fusion | flops 4850712576 | bytes 65011968 | tf_op jit(solution)/shard_map/ijasd,asdb->ijab/dot_general | solution.py:42
  465.8 45.3 %fusion.17 = f32[6,96,64,128]{3,1,0,2:T(8,128)} fusion(f32[64,128,6,96,1]{1,3,4,2,0:T(8,128)} %fusion.2, f32[64,128,6,96,1]{1,3,4,2,0:T(8,128)} %fusion.4, f32[64,128,6,96,1]{1,3,4,2,0:T(8,128)} %fusion.6, f32[64,128,6,96,1]{1,3,4,2,0:T(8,128)} %fusion.8, bf16[64,4,6,96,128]{4,3,2,1,0:T(8,128)(2,1)} %bitcast.104, pred[64,4]{1,0:T(8,128)(4,1)S(1)} %copy-done, ...), kind=kOutput, calls=%fused_computation.30 | convolution fusion | flops 4869586944 | bytes 140509440 | tf_op jit(solution)/shard_map/ijasd,asdb->ijab/dot_general | solution.py:42
  511.1 12.4 copy.86
  523.5 412.4 %all_to_all.36 = f32[6,96,64,128]{3,2,0,1:T(8,128)S(1)} all-to-all(f32[6,96,64,128]{3,2,0,1:T(8,128)S(1)} %copy.86), channel_id=1, replica_groups=mesh['pair'=16,'virt'=2] {'pair'}, dimensions={1} | all-to-all | bytes 37748736 | tf_op jit(solution)/shard_map/all_to_all | solution.py:45
  935.9 7.4 copy.88
  943.4 22.8 %copy.89 = f32[96,6,64,128]{0,2,1,3:T(8,128)} copy(f32[96,6,64,128]{3,2,1,0:T(8,128)} %bitcast.107) | data formatting | bytes 37748736 | tf_op jit(solution)/shard_map/all_to_all | solution.py:45
  966.2 11.9 all-to-all-start.1
  978.1 0.1 dynamic_slice.7
  978.2 0.1 dynamic_slice.6
  978.3 0.1 broadcast_subtract_fusion
  978.5 273.3 %all-to-all-done.1 = f32[96,6,64,128]{0,2,1,3:T(8,128)} async-done(((f32[96,6,64,128]{0,2,1,3:T(8,128)}), f32[96,6,64,128]{0,2,1,3:T(8,128)}, u32[]{:S(2)}, u32[]{:S(2)}) %all-to-all-start.1) | async-done | bytes 18874400 | tf_op jit(solution)/shard_map/all_to_all | solution.py:44
  1251.8 24.9 %copy.91 = f32[96,6,2,64,64]{0,4,3,2,1:T(8,128)} copy(f32[96,6,2,64,64]{0,3,1,4,2:T(8,128)} %bitcast.37) | data formatting | bytes 37748736 | tf_op jit(solution)/shard_map/all_to_all | solution.py:44
  1276.7 22.6 %copy.92 = f32[96,6,128,64]{2,0,1,3:T(8,128)} copy(f32[96,6,128,64]{0,3,2,1:T(8,128)} %bitcast.105) | data formatting | bytes 37748736 | tf_op jit(solution)/shard_map/all_to_all | solution.py:44
  1299.3 16.9 %fusion.16 = bf16[6,96,64,128]{3,1,0,2:T(8,128)(2,1)} fusion(f32[6,96,64,128]{3,1,0,2:T(8,128)} %fusion.17, f32[96,6,128,64]{2,0,1,3:T(8,128)} %copy.92, f32[128]{0:T(128)S(1)} %copy-done.4, f32[6,96,64]{1,0,2:T(8,128)S(1)} %broadcast_subtract_fusion), kind=kLoop, calls=%fused_computation.28 | loop fusion | flops 18874368 | bytes 47333888 | tf_op jit(solution)/shard_map/convert_element_type | solution.py:60
  1316.2 13.5 %copy.93 = bf16[6,96,64,128]{3,2,1,0:T(8,128)(2,1)} copy(bf16[6,96,64,128]{3,1,0,2:T(8,128)(2,1)} %fusion.16) | data formatting | bytes 18874368 | tf_op jit(solution)/shard_map/convert_element_type | solution.py:60
  (19 shorter events, 0.1 us)
Async XLA Ops:
  13.5 207.4 %collective-permute-start = (bf16[6,96,64,128]{3,1,2,0:T(8,128)(2,1)}, bf16[6,96,64,128]{3,1,2,0:T(8,128)(2,1)}, u32[]{:S(2)}, u32[]{:S(2)}) collective-permute-start(bf16[6,96,64,128]{3,1,2,0:T(8,128)(2,1)} %copy.69), channel_id=1, source_target_pairs={{0,1},{2,3},{4,5},{6,7},{8,9},{10,11},{12,13},{14,15},{16,17},{18,... | collective-permute-start | bytes 28311560 | tf_op jit(solution)/shard_map/ppermute | solution.py:15
  22.0 221.1 %collective-permute-start.1 = (bf16[6,96,64,128]{3,1,2,0:T(8,128)(2,1)}, bf16[6,96,64,128]{3,1,2,0:T(8,128)(2,1)}, u32[]{:S(2)}, u32[]{:S(2)}) collective-permute-start(bf16[6,96,64,128]{3,1,2,0:T(8,128)(2,1)} %copy.69), channel_id=1, source_target_pairs={{1,0},{3,2},{5,4},{7,6},{9,8},{11,10},{13,12},{15,14},{17,16},{19,... | collective-permute-start | bytes 28311560 | tf_op jit(solution)/shard_map/ppermute | solution.py:17
  374.2 22.9 %copy-start.1 = (pred[64,4]{1,0:T(8,128)(4,1)S(1)}, pred[64,4]{1,0:T(8,128)(4,1)}, u32[]{:S(2)}) copy-start(pred[64,4]{1,0:T(8,128)(4,1)} %copy.74) | copy-start | bytes 772
  397.1 22.8 %copy-start.2 = (pred[64,4]{1,0:T(8,128)(4,1)S(1)}, pred[64,4]{1,0:T(8,128)(4,1)}, u32[]{:S(2)}) copy-start(pred[64,4]{1,0:T(8,128)(4,1)} %copy.80) | copy-start | bytes 772
  419.9 23.2 %copy-start.3 = (pred[64,4]{1,0:T(8,128)(4,1)S(1)}, pred[64,4]{1,0:T(8,128)(4,1)}, u32[]{:S(2)}) copy-start(pred[64,4]{1,0:T(8,128)(4,1)} %copy.68) | copy-start | bytes 772
  443.0 22.8 %copy-start = (pred[64,4]{1,0:T(8,128)(4,1)S(1)}, pred[64,4]{1,0:T(8,128)(4,1)}, u32[]{:S(2)}) copy-start(pred[64,4]{1,0:T(8,128)(4,1)} %copy.83) | copy-start | bytes 772
  966.2 11.9 copy-start.4
  966.2 12.0 copy-start.5
  966.2 285.6 %all-to-all-start.1 = ((f32[96,6,64,128]{0,2,1,3:T(8,128)}), f32[96,6,64,128]{0,2,1,3:T(8,128)}, u32[]{:S(2)}, u32[]{:S(2)}) async-start(f32[96,6,64,128]{0,2,1,3:T(8,128)} %copy.89), calls=%async_computation.1 | async-start | bytes 50331648 | tf_op jit(solution)/shard_map/all_to_all | solution.py:44
where the time goes:
time: 1340 us; the launch traced here: 1330 us
  waiting for transfers between devices  437 us (33%)
  blocking collectives  412 us (31%)
  local copies, waits for them, and re-layouts  275 us (21%)
  matrix products  137 us (10%)
  other arithmetic  46.8 us (3%)
  starting transfers between devices  21.9 us (2%)
    all_to_all x1, blocking collectives, per_device(): lax.all_to_all(ladder, 'pair', split_axis=1, concat_axis=0, tiled=True)  412 us
    all_to_all x1, waiting for transfers between devices, per_device(): lax.all_to_all(lax.all_to_all(ladder, 'pair', split_axis=1, concat_axis=0...  273 us
    ppermute x1, waiting for transfers between devices, extended(): lax.ppermute(tail, axis, [(i, (i + 1) % count) for i in range(ends)])  164 us
    dot_general x5, matrix products, per_device(): jnp.einsum('ijasd,asdb->ijab', picked, weights, preferred_element_type=jn...  137 us
    gather x5, local copies, waits for them, and re-layouts, per_device(): picked = jnp.take(padded, columns, axis=2)  122 us
    all_to_all x2, local copies, waits for them, and re-layouts, per_device(): lax.all_to_all(lax.all_to_all(ladder, 'pair', split_axis=1, concat_axis=0...  47.5 us
    unnamed x15, local copies, waits for them, and re-layouts  35.8 us
    all_to_all x2, local copies, waits for them, and re-layouts, per_device(): lax.all_to_all(ladder, 'pair', split_axis=1, concat_axis=0, tiled=True)  30.3 us
  transfers between devices with their start and end apart: 3, of which 2 were waited for; matrix products, arithmetic and copies ran while one was open for 4% of the time, Pallas kernels for 0%

commit v1 on v0

--- a/solution.py
+++ b/solution.py
@@ -41,12 +41,20 @@
         weights = masked_weights[:, block_start:block_stop]
         term = jnp.einsum("ijasd,asdb->ijab", picked, weights, preferred_element_type=jnp.float32)
         ladder = term if ladder is None else ladder + term
-    arrived_ladder = lax.all_to_all(
-        lax.all_to_all(ladder, "pair", split_axis=1, concat_axis=0, tiled=True),
-        "virt",
-        split_axis=3,
-        concat_axis=2,
-        tiled=True,
+    arrived_ladder = jnp.concatenate(
+        lax.all_to_all(
+            jnp.stack(
+                jnp.split(
+                    lax.all_to_all(ladder, "pair", split_axis=1, concat_axis=0, tiled=True),
+                    lax.axis_size("virt"),
+                    axis=3,
+                )
+            ),
+            "virt",
+            0,
+            0,
+        ),
+        axis=2,
     )
     partner = jnp.transpose(arrived_ladder, (1, 0, 3, 2))
     occupied_own = lax.dynamic_slice_in_dim(eps_occ, first_row, own_rows)

time: 1340 us -> 1380 us (1.030)
  other arithmetic: 46.8 us -> 76.2 us
  local copies, waits for them, and re-layouts: 275 us -> 292 us
    another operation x0 -> x2, local copies, waits for them, and re-layouts: none -> 47.7 us  [per_device(): jnp.stack(jnp.split(lax.all_to_all(ladder, 'pair', split_axis=1, concat_a...]
    all_to_all x2 -> x0, local copies, waits for them, and re-layouts: 47.5 us -> none  [per_device(): lax.all_to_all(lax.all_to_all(ladder, 'pair', split_axis=1, concat_axis=0...]
    reshape x0 -> x2, local copies, waits for them, and re-layouts: none -> 40.2 us  [per_device(): jnp.concatenate(lax.all_to_all(jnp.stack(jnp.split(lax.all_to_all(ladder,...]
    another operation x0 -> x1, other arithmetic: none -> 29.3 us  [per_device(): jnp.stack(jnp.split(lax.all_to_all(ladder, 'pair', split_axis=1, concat_a...]
    all_to_all x2 -> x1, local copies, waits for them, and re-layouts: 30.3 us -> 7.15 us  [per_device(): lax.all_to_all(ladder, 'pair', split_axis=1, concat_axis=0, tiled=True)]
where the time goes in v1:
time: 1380 us
  waiting for transfers between devices  437 us (32%)
  blocking collectives  413 us (30%)
  local copies, waits for them, and re-layouts  292 us (21%)
  matrix products  137 us (10%)
  other arithmetic  76.2 us (6%)
  starting transfers between devices  21.9 us (2%)
    all_to_all x1, blocking collectives, per_device(): lax.all_to_all(ladder, 'pair', split_axis=1, concat_axis=0, tiled=True)  413 us
    all_to_all x1, waiting for transfers between devices, per_device(): lax.all_to_all(jnp.stack(jnp.split(lax.all_to_all(ladder, 'pair', split_a...  273 us
    ppermute x1, waiting for transfers between devices, extended(): lax.ppermute(tail, axis, [(i, (i + 1) % count) for i in range(ends)])  164 us
    dot_general x5, matrix products, per_device(): jnp.einsum('ijasd,asdb->ijab', picked, weights, preferred_element_type=jn...  137 us
    gather x5, local copies, waits for them, and re-layouts, per_device(): picked = jnp.take(padded, columns, axis=2)  122 us
    another operation x2, local copies, waits for them, and re-layouts, per_device(): jnp.stack(jnp.split(lax.all_to_all(ladder, 'pair', split_axis=1, concat_a...  47.7 us
    reshape x2, local copies, waits for them, and re-layouts, per_device(): jnp.concatenate(lax.all_to_all(jnp.stack(jnp.split(lax.all_to_all(ladder,...  40.2 us
    unnamed x15, local copies, waits for them, and re-layouts  35.8 us
  transfers between devices with their start and end apart: 3, of which 2 were waited for; matrix products, arithmetic and copies ran while one was open for 4% of the time, Pallas kernels for 0%

profile of v1, /device:TPU:0, one launch (start us, length us, event | category | flops | bytes accessed | tf_op | source)
XLA Modules:
  0.0 1376.9 jit_solution(3564846082216690885)
XLA Ops:
  0.0 13.5 copy.69
  13.5 8.6 collective-permute-start
  22.1 1.5 collective-permute-start.1
  23.5 0.7 subtract_add_fusion
  24.3 0.1 copy.75
  24.4 0.1 reshape.127
  24.5 0.1 copy.78
  24.6 0.1 reshape.131
  24.7 0.1 copy.77
  24.8 0.7 copy.74
  25.5 0.1 copy.81
  25.6 0.1 reshape.135
  25.7 0.1 copy.84
  25.8 0.1 reshape.139
  25.9 0.7 copy.80
  26.6 0.1 copy.72
  26.7 0.1 reshape.123
  26.8 0.7 copy.68
  27.5 0.7 copy.83
  28.2 0.7 fusion.25
  29.0 28.2 %broadcast_multiply_fusion = bf16[64,20,128,128]{3,2,1,0:T(8,128)(2,1)} fusion(bf16[64,20,128,128]{3,2,1,0:T(8,128)(2,1)} %param.9, bf16[64,20]{1,0:T(8,128)(2,1)S(1)} %fusion.25), kind=kLoop, calls=%fused_computation.26 | loop fusion | flops 20971520 | bytes 83888640 | tf_op jit(solution)/shard_map/mul | solution.py:33
  57.2 163.7 %collective-permute-done = bf16[6,96,64,128]{3,1,2,0:T(8,128)(2,1)} collective-permute-done((bf16[6,96,64,128]{3,1,2,0:T(8,128)(2,1)}, bf16[6,96,64,128]{3,1,2,0:T(8,128)(2,1)}, u32[]{:S(2)}, u32[]{:S(2)}) %collective-permute-start) | collective-permute-done | bytes 9437216 | tf_op jit(solution)/shard_map/ppermute | solution.py:15
  220.9 9.0 constant_dynamic-update-slice_fusion.2
  229.9 13.3 constant_dynamic-update-slice_fusion.1
  243.2 9.0 constant_dynamic-update-slice_fusion
  252.2 24.5 %gather_fusion.2 = bf16[256,6,96,128]{3,2,1,0:T(8,128)(2,1)} fusion(bf16[6,96,192,128]{3,1,2,0:T(8,128)(2,1)} %constant_dynamic-update-slice_fusion, s32[1024]{0:T(1024)S(1)} %get-tuple-element.20), kind=kCustom, calls=%fused_computation.2.clone | custom fusion | bytes 75498496 | tf_op jit(solution)/shard_map/jit(_take)/gather | solution.py:40
  276.7 24.5 %gather_fusion.1 = bf16[256,6,96,128]{3,2,1,0:T(8,128)(2,1)} fusion(bf16[6,96,192,128]{3,1,2,0:T(8,128)(2,1)} %constant_dynamic-update-slice_fusion, s32[1024]{0:T(1024)S(1)} %get-tuple-element.21), kind=kCustom, calls=%fused_computation.1.clone | custom fusion | bytes 75498496 | tf_op jit(solution)/shard_map/jit(_take)/gather | solution.py:40
  301.2 24.3 %gather_fusion.3 = bf16[256,6,96,128]{3,2,1,0:T(8,128)(2,1)} fusion(bf16[6,96,192,128]{3,1,2,0:T(8,128)(2,1)} %constant_dynamic-update-slice_fusion, s32[1024]{0:T(1024)S(1)} %get-tuple-element.19), kind=kCustom, calls=%fused_computation.3.clone | custom fusion | bytes 75498496 | tf_op jit(solution)/shard_map/jit(_take)/gather | solution.py:40
  325.5 24.3 %gather_fusion = bf16[256,6,96,128]{3,2,1,0:T(8,128)(2,1)} fusion(bf16[6,96,192,128]{3,1,2,0:T(8,128)(2,1)} %constant_dynamic-update-slice_fusion, s32[1024]{0:T(1024)S(1)} %pad_clamp_fusion.4), kind=kCustom, calls=%fused_computation.clone | custom fusion | bytes 75498496 | tf_op jit(solution)/shard_map/jit(_take)/gather | solution.py:40
  349.8 24.4 %gather_fusion.4 = bf16[256,6,96,128]{3,2,1,0:T(8,128)(2,1)} fusion(bf16[6,96,192,128]{3,1,2,0:T(8,128)(2,1)} %constant_dynamic-update-slice_fusion, s32[1024]{0:T(1024)S(1)} %get-tuple-element.18), kind=kCustom, calls=%fused_computation.4.clone | custom fusion | bytes 75498496 | tf_op jit(solution)/shard_map/jit(_take)/gather | solution.py:40
  374.3 22.9 %fusion.4 = f32[64,128,6,96,1]{1,3,4,2,0:T(8,128)} fusion(bf16[64,4,6,96,128]{4,3,2,1,0:T(8,128)(2,1)} %bitcast.112, pred[64,4]{1,0:T(8,128)(4,1)S(1)} %copy.77, bf16[64,20,128,128]{3,2,1,0:T(8,128)(2,1)} %broadcast_multiply_fusion), kind=kOutput, calls=%fused_computation.10 | convolution fusion | flops 4850712576 | bytes 65011968 | tf_op jit(solution)/shard_map/ijasd,asdb->ijab/dot_general | solution.py:42
  397.1 22.8 %fusion.6 = f32[64,128,6,96,1]{1,3,4,2,0:T(8,128)} fusion(bf16[64,4,6,96,128]{4,3,2,1,0:T(8,128)(2,1)} %bitcast.113, pred[64,4]{1,0:T(8,128)(4,1)S(1)} %copy-done.1, bf16[64,20,128,128]{3,2,1,0:T(8,128)(2,1)} %broadcast_multiply_fusion), kind=kOutput, calls=%fused_computation.12 | convolution fusion | flops 4850712576 | bytes 65011968 | tf_op jit(solution)/shard_map/ijasd,asdb->ijab/dot_general | solution.py:42
  419.9 23.1 %fusion.2 = f32[64,128,6,96,1]{1,3,4,2,0:T(8,128)} fusion(bf16[64,4,6,96,128]{4,3,2,1,0:T(8,128)(2,1)} %bitcast.111, pred[64,4]{1,0:T(8,128)(4,1)S(1)} %copy-done.2, bf16[64,20,128,128]{3,2,1,0:T(8,128)(2,1)} %broadcast_multiply_fusion), kind=kOutput, calls=%fused_computation.8 | convolution fusion | flops 4850712576 | bytes 65011968 | tf_op jit(solution)/shard_map/ijasd,asdb->ijab/dot_general | solution.py:42
  443.1 22.8 %fusion.8 = f32[64,128,6,96,1]{1,3,4,2,0:T(8,128)} fusion(bf16[64,4,6,96,128]{4,3,2,1,0:T(8,128)(2,1)} %bitcast.110, pred[64,4]{1,0:T(8,128)(4,1)S(1)} %copy-done.3, bf16[64,20,128,128]{3,2,1,0:T(8,128)(2,1)} %broadcast_multiply_fusion), kind=kOutput, calls=%fused_computation.14 | convolution fusion | flops 4850712576 | bytes 65011968 | tf_op jit(solution)/shard_map/ijasd,asdb->ijab/dot_general | solution.py:42
  465.9 45.4 %fusion.17 = f32[6,96,64,128]{3,1,0,2:T(8,128)} fusion(f32[64,128,6,96,1]{1,3,4,2,0:T(8,128)} %fusion.2, f32[64,128,6,96,1]{1,3,4,2,0:T(8,128)} %fusion.4, f32[64,128,6,96,1]{1,3,4,2,0:T(8,128)} %fusion.6, f32[64,128,6,96,1]{1,3,4,2,0:T(8,128)} %fusion.8, bf16[64,4,6,96,128]{4,3,2,1,0:T(8,128)(2,1)} %bitcast.106, pred[64,4]{1,0:T(8,128)(4,1)S(1)} %copy-done, ...), kind=kOutput, calls=%fused_computation.33 | convolution fusion | flops 4869586944 | bytes 140509440 | tf_op jit(solution)/shard_map/ijasd,asdb->ijab/dot_general | solution.py:42
  511.3 12.4 copy.86
  523.7 412.7 %all_to_all.23 = f32[6,96,64,128]{3,2,0,1:T(8,128)} all-to-all(f32[6,96,64,128]{3,2,0,1:T(8,128)S(1)} %copy.86), channel_id=1, replica_groups=mesh['pair'=16,'virt'=2] {'pair'}, dimensions={1} | all-to-all | bytes 37748736 | tf_op jit(solution)/shard_map/all_to_all | solution.py:48
  936.4 7.1 copy.88
  943.5 13.4 slice_bitcast_fusion.1
  956.9 29.3 %pad_maximum_fusion = f32[2,96,6,64,64]{4,3,2,1,0:T(8,128)} fusion(f32[1,96,6,64,64]{4,3,2,1,0:T(8,128)} %get-tuple-element.7, f32[1,96,6,64,64]{4,3,2,1,0:T(8,128)} %get-tuple-element.6), kind=kLoop, calls=%fused_computation.5 | loop fusion | flops 4718592 | bytes 37748736 | tf_op jit(solution)/shard_map/stack | solution.py:46
  986.2 34.3 %copy.89 = f32[2,96,6,64,64]{1,4,3,2,0:T(8,128)} copy(f32[2,96,6,64,64]{4,3,2,1,0:T(8,128)} %pad_maximum_fusion) | data formatting | bytes 37748736 | tf_op jit(solution)/shard_map/stack | solution.py:46
  1020.6 11.9 all-to-all-start.1
  1032.7 0.1 broadcast_subtract_fusion
  1032.8 273.3 %all-to-all-done.1 = f32[2,96,6,64,64]{1,4,3,2,0:T(8,128)} async-done(((f32[2,96,6,64,64]{1,4,3,2,0:T(8,128)}), f32[2,96,6,64,64]{1,4,3,2,0:T(8,128)}, u32[]{:S(2)}, u32[]{:S(2)}) %all-to-all-start.1) | async-done | bytes 18874400 | tf_op jit(solution)/shard_map/all_to_all | solution.py:45
  1306.1 17.6 %copy.90 = f32[96,6,2,64,64]{0,4,3,2,1:T(8,128)} copy(f32[96,6,2,64,64]{0,4,3,1,2:T(8,128)} %bitcast.37) | data formatting | bytes 37748736 | tf_op jit(solution)/shard_map/reshape | solution.py:44
  1323.7 22.6 %copy.91 = f32[96,6,128,64]{2,0,1,3:T(8,128)} copy(f32[96,6,128,64]{0,3,2,1:T(8,128)} %bitcast.108) | data formatting | bytes 37748736 | tf_op jit(solution)/shard_map/reshape | solution.py:44
  1346.3 16.9 %fusion.16 = bf16[6,96,64,128]{3,1,0,2:T(8,128)(2,1)} fusion(f32[6,96,64,128]{3,1,0,2:T(8,128)} %fusion.17, f32[96,6,128,64]{2,0,1,3:T(8,128)} %copy.91, f32[128]{0:T(128)S(1)} %copy-done.4, f32[6,96,64]{1,0,2:T(8,128)S(1)} %broadcast_subtract_fusion), kind=kLoop, calls=%fused_computation.31 | loop fusion | flops 18874368 | bytes 47333888 | tf_op jit(solution)/shard_map/convert_element_type | solution.py:68
  1363.2 13.5 copy.92
  (21 shorter events, 0.3 us)
Async XLA Ops:
  13.5 207.4 %collective-permute-start = (bf16[6,96,64,128]{3,1,2,0:T(8,128)(2,1)}, bf16[6,96,64,128]{3,1,2,0:T(8,128)(2,1)}, u32[]{:S(2)}, u32[]{:S(2)}) collective-permute-start(bf16[6,96,64,128]{3,1,2,0:T(8,128)(2,1)} %copy.69), channel_id=1, source_target_pairs={{0,1},{2,3},{4,5},{6,7},{8,9},{10,11},{12,13},{14,15},{16,17},{18,... | collective-permute-start | bytes 28311560 | tf_op jit(solution)/shard_map/ppermute | solution.py:15
  22.1 221.1 %collective-permute-start.1 = (bf16[6,96,64,128]{3,1,2,0:T(8,128)(2,1)}, bf16[6,96,64,128]{3,1,2,0:T(8,128)(2,1)}, u32[]{:S(2)}, u32[]{:S(2)}) collective-permute-start(bf16[6,96,64,128]{3,1,2,0:T(8,128)(2,1)} %copy.69), channel_id=1, source_target_pairs={{1,0},{3,2},{5,4},{7,6},{9,8},{11,10},{13,12},{15,14},{17,16},{19,... | collective-permute-start | bytes 28311560 | tf_op jit(solution)/shard_map/ppermute | solution.py:17
  374.3 22.9 %copy-start.1 = (pred[64,4]{1,0:T(8,128)(4,1)S(1)}, pred[64,4]{1,0:T(8,128)(4,1)}, u32[]{:S(2)}) copy-start(pred[64,4]{1,0:T(8,128)(4,1)} %copy.74) | copy-start | bytes 772
  397.1 22.8 %copy-start.2 = (pred[64,4]{1,0:T(8,128)(4,1)S(1)}, pred[64,4]{1,0:T(8,128)(4,1)}, u32[]{:S(2)}) copy-start(pred[64,4]{1,0:T(8,128)(4,1)} %copy.80) | copy-start | bytes 772
  419.9 23.2 %copy-start.3 = (pred[64,4]{1,0:T(8,128)(4,1)S(1)}, pred[64,4]{1,0:T(8,128)(4,1)}, u32[]{:S(2)}) copy-start(pred[64,4]{1,0:T(8,128)(4,1)} %copy.68) | copy-start | bytes 772
  443.1 22.8 %copy-start = (pred[64,4]{1,0:T(8,128)(4,1)S(1)}, pred[64,4]{1,0:T(8,128)(4,1)}, u32[]{:S(2)}) copy-start(pred[64,4]{1,0:T(8,128)(4,1)} %copy.83) | copy-start | bytes 772
  1020.6 11.9 copy-start.4
  1020.6 12.0 copy-start.5
  1020.6 285.6 %all-to-all-start.1 = ((f32[2,96,6,64,64]{1,4,3,2,0:T(8,128)}), f32[2,96,6,64,64]{1,4,3,2,0:T(8,128)}, u32[]{:S(2)}, u32[]{:S(2)}) async-start(f32[2,96,6,64,64]{1,4,3,2,0:T(8,128)} %copy.89), calls=%async_computation.1 | async-start | bytes 50331648 | tf_op jit(solution)/shard_map/all_to_all | solution.py:45
